TPU v7x, 512 devices: a whole 4x4x16 slice. The times are simulated.
512 devices in a mesh: mp: 8 (over z_lo, core), feat: 64 (over x, z_hi, y).
Axes of the slice: x: 4, y: 4, z: 16 (z_hi: 4, z_lo: 4; z = z_hi * 4 + z_lo), core: 2. Of those that a mesh axis runs over, the one named last changes fastest.
Arguments:
- target_ids: int32 [16], replicated, may hold values from 0 to 127999
- target_pos: int32 [16], replicated, may hold values from 24 to 47
- unembed: bfloat16 [128000, 2304], P(('mp', 'feat')), may hold values from -6 to 6
- attn_weights: float32 [8, 16, 48, 48], P('mp'), may hold values from 0.02 to 1
- inv_rms: float32 [16, 48], replicated, may hold values from 0.5 to 2
- norm_gain: float32 [2304], replicated, may hold values from 0.1 to 1.9
- w_value: bfloat16 [4, 2304, 256], P(None, 'mp'), may hold values from -0.125 to 0.125
- w_out: bfloat16 [8, 256, 2304], P('mp'), may hold values from -0.375 to 0.375
- decoder: bfloat16 [2, 98304, 2304], P(None, ('mp', 'feat')), may hold values from -0.125 to 0.125
- activation: bfloat16 [16, 48, 98304], P(None, None, ('mp', 'feat')), may hold values from 0.5 to 4
- active: int32 [16, 48, 98304], P(None, None, ('mp', 'feat')), may hold values 0 or 1
Outputs:
- attribution: float32 [16, 48, 98304], P(None, None, ('mp', 'feat'))
All inputs are finite; a program needn't handle non-finite values. No bound on the sum of `active` on one device may be relied on, other than what follows from the above.
Results may differ from a plain program's by a relative error of at most 0.0035.
Values may be sent and summed in bfloat16 or wider, within the bound.
No kernel may reach another device: no remote copies, remote signals or barrier semaphores. Data moves between devices by JAX's collectives and lax.ppermute only.
A program may use at most 64 MiB of HBM per device.

v0:
```python
import jax
import jax.numpy as jnp
from jax import lax
from jax.sharding import PartitionSpec as P


def on_device(
    target_ids,
    target_pos,
    unembed,
    attn_weights,
    inv_rms,
    norm_gain,
    w_value,
    w_out,
    decoder,
    activation,
    active,
):
    vocab_rows = unembed.shape[0]
    model_width = unembed.shape[1]
    targets = target_ids.shape[0]
    positions = inv_rms.shape[1]
    local_heads = w_out.shape[0]
    kv_heads = w_value.shape[0]
    column_count = w_value.shape[1]
    row_count = targets * positions
    own_rows = row_count // lax.axis_size("feat")
    device_rank = lax.axis_index("mp") * lax.axis_size("feat") + lax.axis_index("feat")
    first_row = device_rank * vocab_rows
    picker = (
        target_ids[:, None] == first_row + jnp.arange(vocab_rows, dtype=jnp.int32)[None, :]
    ).astype(jnp.bfloat16)
    direction = lax.psum(
        jnp.dot(picker, unembed, preferred_element_type=jnp.float32), ("mp", "feat")
    )
    placing = (jnp.arange(positions, dtype=jnp.int32)[None, :] == target_pos[:, None]).astype(
        jnp.float32
    )
    upper = (placing[:, :, None] * direction[:, None, :]).reshape(row_count, model_width)
    lowered_top = upper.astype(jnp.bfloat16)
    row_start = lax.axis_index("feat") * own_rows
    column_start = lax.axis_index("mp") * column_count
    index_pos = jnp.arange(positions, dtype=jnp.int32)
    causal = (index_pos[:, None] >= index_pos[None, :]).astype(jnp.float32)
    weights = attn_weights * causal
    pattern = weights / jnp.sum(weights, axis=-1, keepdims=True)
    flipped = jnp.swapaxes(pattern, 2, 3).reshape(local_heads, row_count, positions)
    own_pattern = lax.dynamic_slice_in_dim(flipped, row_start, own_rows, 1)
    row_group = (row_start + jnp.arange(own_rows, dtype=jnp.int32)) // positions
    group_pick = (row_group[:, None] == jnp.arange(targets, dtype=jnp.int32)[None, :]).astype(
        jnp.float32
    )
    block_pattern = (own_pattern[:, :, None, :] * group_pick[None, :, :, None]).reshape(
        local_heads, own_rows, row_count
    )
    mixed = jnp.einsum(
        "hrq,qd->hrd",
        block_pattern,
        lowered_top.astype(jnp.float32),
        precision=lax.Precision.HIGHEST,
    ).astype(jnp.bfloat16)
    spread = jnp.einsum("hrd,hkd->hrk", mixed, w_out, preferred_element_type=jnp.float32).astype(
        jnp.bfloat16
    )
    all_spread = lax.all_gather(spread, "mp", axis=0, tiled=True)
    group_size = local_heads * lax.axis_size("mp") // kv_heads
    value_heads = jnp.repeat(w_value, group_size, axis=0)
    heads_sum = jnp.einsum(
        "hrk,hck->rc", all_spread, value_heads, preferred_element_type=jnp.float32
    )
    upper_rows = lax.dynamic_slice_in_dim(upper, row_start, own_rows, 0)
    upper_block = lax.dynamic_slice_in_dim(upper_rows, column_start, column_count, 1)
    scale_rows = lax.dynamic_slice_in_dim(inv_rms.reshape(row_count, 1), row_start, own_rows, 0)
    gain_columns = lax.dynamic_slice_in_dim(norm_gain, column_start, column_count, 0)
    below_block = upper_block + scale_rows * gain_columns[None, :] * heads_sum
    lowered_block = below_block.astype(jnp.bfloat16)
    top_scores = jnp.einsum(
        "rd,fd->rf", lowered_top, decoder[1], preferred_element_type=jnp.float32
    )
    tall_block = lax.all_gather(lowered_block, "feat", axis=0, tiled=True)
    lowered_bottom = lax.all_gather(tall_block, "mp", axis=1, tiled=True)
    bottom_scores = jnp.einsum(
        "rd,fd->rf", lowered_bottom, decoder[0], preferred_element_type=jnp.float32
    )
    scores = bottom_scores + top_scores
    feature_count = decoder.shape[1]
    attribution = (
        activation.astype(jnp.float32).reshape(row_count, feature_count)
        * active.reshape(row_count, feature_count).astype(jnp.float32)
        * scores
    )
    return attribution.reshape(targets, positions, feature_count)


def solution(mesh):
    in_specs = (
        P(),
        P(),
        P(("mp", "feat"), None),
        P("mp", None, None, None),
        P(),
        P(),
        P(None, "mp", None),
        P("mp", None, None),
        P(None, ("mp", "feat"), None),
        P(None, None, ("mp", "feat")),
        P(None, None, ("mp", "feat")),
    )
    out_specs = P(None, None, ("mp", "feat"))
    return jax.shard_map(
        on_device, mesh=mesh, in_specs=in_specs, out_specs=out_specs, check_vma=False
    )
```

profile of v0, /device:TPU:2, one launch (start us, length us, event | category | flops | bytes accessed | tf_op | source)
XLA Modules:
  0.0 761.0 jit_solution(12552327615252992566)
XLA Ops:
  6.5 0.0 copy-start
  6.5 0.0 copy-start.7
  6.5 0.0 copy-start.6
  6.5 0.0 all-reduce.2.cloned.1.call-start
  6.6 1.2 copy-done
  7.8 0.0 copy-start.1
  7.8 1.7 fusion.23
  9.5 0.0 all-reduce.2.cloned.1.call-update
  9.6 0.0 all-gather.5.cloned.1.call-start
  9.7 1.2 multiply_reduce_fusion
  10.8 1.2 divide_bitcast_fusion
  12.0 0.1 copy.21
  12.1 0.2 reshape.175
  12.3 0.1 constant_dynamic-slice_fusion
  12.4 0.1 copy.22
  12.5 0.0 copy-done.7
  12.5 0.1 fusion.27
  12.6 0.1 reshape.179
  12.7 0.0 copy-done.6
  12.7 0.1 reshape.174
  12.7 0.8 dynamic_slice.15
  13.5 0.1 dynamic-slice
  13.6 0.1 dynamic-slice_bitcast_fusion
  13.7 450.9 %all-reduce.2.cloned.1.call-done = f32[16,2304]{1,0:T(8,128)} async-done(((f32[16,2304]{1,0:T(8,128)}), f32[16,2304]{1,0:T(8,128)}) %all-reduce.2.cloned.1.call-update) | async-done | bytes 147472 | tf_op jit(solution)/shard_map/psum | solution.py:34
  464.6 0.0 copy-start.4
  464.6 2.9 fusion
  467.5 0.0 copy-done.1
  467.5 0.4 fusion.11
  467.8 14.0 %all-gather.1 = bf16[8,12,256]{2,1,0:T(8,128)(2,1)S(1)} all-gather(bf16[1,12,256]{2,1,0:T(8,128)(2,1)S(1)} %fusion.11), channel_id=2, replica_groups=mesh['mp'=8,'feat'=64] {'mp'}, dimensions={0}, use_global_device_ids=true | all-gather | bytes 55296 | tf_op jit(solution)/shard_map/all_gather | solution.py:66
  481.9 0.0 copy-done.4
  481.9 0.0 copy-start.3
  481.9 0.5 mul.102
  482.4 0.0 copy-start.2
  482.4 0.5 copy-done.3
  482.9 0.1 broadcast_in_dim.2
  483.0 0.4 fusion.7
  483.5 202.2 %all-gather.2 = bf16[64,12,288]{2,1,0:T(8,128)(2,1)S(1)} all-gather(bf16[1,12,288]{2,1,0:T(8,128)(2,1)S(1)} %fusion.7), channel_id=1, replica_groups=mesh['mp'=8,'feat'=64] {'feat'}, dimensions={0}, use_global_device_ids=true | all-gather | bytes 449280 | tf_op jit(solution)/shard_map/all_gather | solution.py:81
  685.7 0.3 reshape.184
  686.0 1.0 copy.23
  687.0 0.0 all-gather.5.cloned.1.call-update
  687.0 0.0 copy-done.2
  687.0 1.1 convert_multiply_fusion
  688.1 0.2 copy.24
  688.4 0.0 copy-start.5
  688.4 0.5 multiply_convert_fusion
  688.9 0.9 copy-done.5
  689.9 1.3 fusion.14
  691.2 58.7 %all-gather.5.cloned.1.call-done = bf16[768,2304]{0,1:T(8,128)(2,1)} async-done(((bf16[768,288]{0,1:T(8,128)(2,1)}), bf16[768,2304]{0,1:T(8,128)(2,1)}) %all-gather.5.cloned.1.call-update) | async-done | bytes 3538960 | tf_op jit(solution)/shard_map/all_gather | solution.py:82
  749.9 3.1 fusion.1
  753.0 1.1 copy.25
  (4 shorter events, 0.0 us)
Async XLA Ops:
  6.5 1.3 copy-start
  6.5 6.0 copy-start.7
  6.5 6.1 copy-start.6
  6.5 458.1 %all-reduce.2.cloned.1.call-start = ((), (), s32[]{:S(2)}) async-start(), calls=%async_computation | async-start | bytes 294912 | tf_op jit(solution)/shard_map/psum | solution.py:34
  7.8 459.7 %copy-start.1 = (bf16[1,256,2304]{2,1,0:T(8,128)(2,1)S(1)}, bf16[1,256,2304]{2,1,0:T(8,128)(2,1)}, u32[]{:S(2)}) copy-start(bf16[1,256,2304]{2,1,0:T(8,128)(2,1)} %param.18) | copy-start | bytes 3538948
  9.6 740.3 %all-gather.5.cloned.1.call-start = ((), (), s32[]{:S(2)}) async-start(), calls=%async_computation.1 | async-start | bytes 3981312 | tf_op jit(solution)/shard_map/all_gather | solution.py:82
  464.6 17.3 %copy-start.4 = (f32[16,2304]{1,0:T(8,128)S(1)}, f32[16,2304]{1,0:T(8,128)}, u32[]{:S(2)}) copy-start(f32[16,2304]{1,0:T(8,128)} %all-reduce.2.cloned.1.call-done) | copy-start | bytes 442372
  481.9 1.1 copy-start.3
  482.4 204.6 %copy-start.2 = (s32[16,48,192]{2,1,0:T(8,128)S(1)}, s32[16,48,192]{2,1,0:T(8,128)}, u32[]{:S(2)}) copy-start(s32[16,48,192]{2,1,0:T(8,128)} %param.21) | copy-start | bytes 1769476
  688.4 1.5 copy-start.5
Sparse Core Ops, SparseCore 0:
  12.8 451.7 all-reduce.1
  687.1 62.7 all-gather.4
where the time goes:
time: 761 us
  waiting for transfers between devices  510 us (67%)
  blocking collectives  216 us (28%)
  between operations  13.6 us (2%)
  matrix products  9.86 us (1%)
    psum x1, waiting for transfers between devices, on_device(): lax.psum(jnp.dot(picker, unembed, preferred_element_type=jnp.float32), ('...  451 us
    all_gather x1, blocking collectives, on_device(): tall_block = lax.all_gather(lowered_block, 'feat', axis=0, tiled=True)  202 us
    all_gather x1, waiting for transfers between devices, on_device(): lowered_bottom = lax.all_gather(tall_block, 'mp', axis=1, tiled=True)  58.7 us
  transfers between devices with their start and end apart: 2, of which 2 were waited for; matrix products, arithmetic and copies ran while one was open for 1% of the time, Pallas kernels for 0%

commit v1 on v0

--- a/solution.py
+++ b/solution.py
@@ -2,6 +2,8 @@
 import jax.numpy as jnp
 from jax import lax
 from jax.sharding import PartitionSpec as P
+
+attach_the_levels_all = lambda array_in: lax.psum(lax.psum(array_in, "mp"), "feat")
 
 
 def on_device(
@@ -31,9 +33,7 @@
     picker = (
         target_ids[:, None] == first_row + jnp.arange(vocab_rows, dtype=jnp.int32)[None, :]
     ).astype(jnp.bfloat16)
-    direction = lax.psum(
-        jnp.dot(picker, unembed, preferred_element_type=jnp.float32), ("mp", "feat")
-    )
+    direction = attach_the_levels_all(jnp.dot(picker, unembed, preferred_element_type=jnp.float32))
     placing = (jnp.arange(positions, dtype=jnp.int32)[None, :] == target_pos[:, None]).astype(
         jnp.float32
     )

time: 761 us -> 1160 us (1.52)
  waiting for transfers between devices: 510 us -> 904 us
    psum x1 -> x2, waiting for transfers between devices: 451 us -> 820 us  [the longest x1 740 us: lax.psum(lax.psum(array_in, 'mp'), 'feat')]
    all_gather x1, waiting for transfers between devices: 58.7 us -> 84.1 us  [on_device(): lowered_bottom = lax.all_gather(tall_block, 'mp', axis=1, tiled=True)]
  transfers between devices with their start and end apart: 2 -> 3, of which waited for: 2 -> 3; matrix products, arithmetic and copies ran while one was open for 1% -> 1% of each run, Pallas kernels for 0% -> 0%
where the time goes in v1:
time: 1160 us
  waiting for transfers between devices  904 us (78%)
  blocking collectives  218 us (19%)
  between operations  13.3 us (1%)
    psum x1, waiting for transfers between devices, lax.psum(lax.psum(array_in, 'mp'), 'feat')  740 us
    all_gather x1, blocking collectives, on_device(): tall_block = lax.all_gather(lowered_block, 'feat', axis=0, tiled=True)  204 us
    all_gather x1, waiting for transfers between devices, on_device(): lowered_bottom = lax.all_gather(tall_block, 'mp', axis=1, tiled=True)  84.1 us
    psum x1, waiting for transfers between devices, lax.psum(array_in, 'mp')  80 us
  transfers between devices with their start and end apart: 3, of which 3 were waited for; matrix products, arithmetic and copies ran while one was open for 1% of the time, Pallas kernels for 0%

profile of v1, /device:TPU:2, one launch (start us, length us, event | category | flops | bytes accessed | tf_op | source)
XLA Modules:
  0.0 1157.5 jit_solution(6221271685507907421)
XLA Ops:
  6.5 0.0 copy-start
  6.5 0.0 copy-start.7
  6.5 0.0 copy-start.6
  6.5 0.0 all-reduce.3.cloned.1.call-start
  6.6 1.2 copy-done
  7.8 1.6 fusion.23
  9.4 0.0 copy-start.1
  9.4 0.0 all-reduce.3.cloned.1.call-update
  9.5 0.0 all-reduce.5.cloned.1.call-start
  9.6 1.2 multiply_reduce_fusion
  10.8 1.2 divide_bitcast_fusion
  12.0 0.1 copy.21
  12.1 0.2 reshape.175
  12.3 0.0 copy-done.7
  12.3 0.1 fusion.27
  12.4 80.0 %all-reduce.3.cloned.1.call-done = f32[16,2304]{1,0:T(8,128)} async-done(((f32[16,2304]{1,0:T(8,128)}), f32[16,2304]{1,0:T(8,128)}) %all-reduce.3.cloned.1.call-update) | async-done | bytes 147472 | tf_op jit(solution)/shard_map/psum | solution.py:6
  92.4 0.0 all-reduce.5.cloned.1.call-update
  92.5 0.0 all-gather.5.cloned.1.call-start
  92.5 0.1 constant_dynamic-slice_fusion
  92.6 0.1 copy.22
  92.7 0.1 reshape.179
  92.8 0.0 copy-done.6
  92.8 0.1 reshape.174
  92.9 0.8 dynamic_slice.15
  93.6 0.1 dynamic-slice
  93.7 0.1 dynamic-slice_bitcast_fusion
  93.8 740.2 %all-reduce.5.cloned.1.call-done = f32[16,2304]{1,0:T(8,128)} async-done(((f32[16,2304]{1,0:T(8,128)}), f32[16,2304]{1,0:T(8,128)}) %all-reduce.5.cloned.1.call-update) | async-done | bytes 147472 | tf_op jit(solution)/shard_map/psum | solution.py:6
  834.0 0.0 copy-start.4
  834.0 2.9 fusion
  836.9 0.0 copy-done.1
  836.9 0.4 fusion.11
  837.3 14.0 %all-gather.1 = bf16[8,12,256]{2,1,0:T(8,128)(2,1)S(1)} all-gather(bf16[1,12,256]{2,1,0:T(8,128)(2,1)S(1)} %fusion.11), channel_id=2, replica_groups=mesh['mp'=8,'feat'=64] {'mp'}, dimensions={0}, use_global_device_ids=true | all-gather | bytes 55296 | tf_op jit(solution)/shard_map/all_gather | solution.py:66
  851.3 0.0 copy-done.4
  851.3 0.0 copy-start.3
  851.3 0.5 mul.102
  851.8 0.0 copy-start.2
  851.9 0.5 copy-done.3
  852.4 0.1 broadcast_in_dim.2
  852.4 0.4 fusion.7
  852.9 204.3 %all-gather.2 = bf16[64,12,288]{2,1,0:T(8,128)(2,1)S(1)} all-gather(bf16[1,12,288]{2,1,0:T(8,128)(2,1)S(1)} %fusion.7), channel_id=1, replica_groups=mesh['mp'=8,'feat'=64] {'feat'}, dimensions={0}, use_global_device_ids=true | all-gather | bytes 449280 | tf_op jit(solution)/shard_map/all_gather | solution.py:81
  1057.2 0.3 reshape.184
  1057.5 1.0 copy.23
  1058.5 0.0 all-gather.5.cloned.1.call-update
  1058.5 0.0 copy-done.2
  1058.5 1.1 convert_multiply_fusion
  1059.6 0.2 copy.24
  1059.8 0.0 copy-start.5
  1059.9 0.5 multiply_convert_fusion
  1060.4 0.9 copy-done.5
  1061.3 1.3 fusion.14
  1062.6 84.1 %all-gather.5.cloned.1.call-done = bf16[768,2304]{0,1:T(8,128)(2,1)} async-done(((bf16[768,288]{0,1:T(8,128)(2,1)}), bf16[768,2304]{0,1:T(8,128)(2,1)}) %all-gather.5.cloned.1.call-update) | async-done | bytes 3538960 | tf_op jit(solution)/shard_map/all_gather | solution.py:82
  1146.7 3.1 fusion.1
  1149.8 1.1 copy.25
  (4 shorter events, 0.0 us)
Async XLA Ops:
  6.5 1.3 copy-start
  6.5 5.8 copy-start.7
  6.5 86.2 %copy-start.6 = (f32[16,48]{1,0:T(8,128)S(1)}, f32[16,48]{1,0:T(8,128)}, u32[]{:S(2)}) copy-start(f32[16,48]{1,0:T(8,128)} %param.15) | copy-start | bytes 9220
  6.5 85.9 %all-reduce.3.cloned.1.call-start = ((), (), s32[]{:S(2)}) async-start(), calls=%async_computation | async-start | bytes 294912 | tf_op jit(solution)/shard_map/psum | solution.py:6
  9.4 827.4 %copy-start.1 = (bf16[1,256,2304]{2,1,0:T(8,128)(2,1)S(1)}, bf16[1,256,2304]{2,1,0:T(8,128)(2,1)}, u32[]{:S(2)}) copy-start(bf16[1,256,2304]{2,1,0:T(8,128)(2,1)} %param.18) | copy-start | bytes 3538948
  9.5 824.5 %all-reduce.5.cloned.1.call-start = ((), (), s32[]{:S(2)}) async-start(), calls=%async_computation.1 | async-start | bytes 294912 | tf_op jit(solution)/shard_map/psum | solution.py:6
  92.5 1054.2 %all-gather.5.cloned.1.call-start = ((), (), s32[]{:S(2)}) async-start(), calls=%async_computation.2 | async-start | bytes 3981312 | tf_op jit(solution)/shard_map/all_gather | solution.py:82
  834.0 17.3 %copy-start.4 = (f32[16,2304]{1,0:T(8,128)S(1)}, f32[16,2304]{1,0:T(8,128)}, u32[]{:S(2)}) copy-start(f32[16,2304]{1,0:T(8,128)} %all-reduce.5.cloned.1.call-done) | copy-start | bytes 442372
  851.3 1.1 copy-start.3
  851.8 206.6 %copy-start.2 = (s32[16,48,192]{2,1,0:T(8,128)S(1)}, s32[16,48,192]{2,1,0:T(8,128)}, u32[]{:S(2)}) copy-start(s32[16,48,192]{2,1,0:T(8,128)} %param.21) | copy-start | bytes 1769476
  1059.8 1.5 copy-start.5
Sparse Core Ops, SparseCore 0:
  10.3 82.1 all-reduce.2
  95.6 738.3 all-reduce.4
  1058.6 88.0 all-gather.4

commit v2 on v0

--- a/solution.py
+++ b/solution.py
@@ -79,7 +79,15 @@
         "rd,fd->rf", lowered_top, decoder[1], preferred_element_type=jnp.float32
     )
     tall_block = lax.all_gather(lowered_block, "feat", axis=0, tiled=True)
-    lowered_bottom = lax.all_gather(tall_block, "mp", axis=1, tiled=True)
+    lowered_bottom = jnp.concatenate(
+        lax.all_to_all(
+            jnp.stack([tall_block] * lax.axis_size("mp"), 0),
+            axis_name="mp",
+            split_axis=0,
+            concat_axis=0,
+        ),
+        1,
+    )
     bottom_scores = jnp.einsum(
         "rd,fd->rf", lowered_bottom, decoder[0], preferred_element_type=jnp.float32
     )

time: 761 us -> 806 us (1.059)
  the two profiles are of different devices: /device:TPU:2 before, /device:TPU:1 now
where the time goes in v2:
time: 806 us
  waiting for transfers between devices  529 us (66%)
  blocking collectives  209 us (26%)
  starting transfers between devices  32.5 us (4%)
  between operations  13.5 us (2%)
  matrix products  9.86 us (1%)
  local copies, waits for them, and re-layouts  8.86 us (1%)
    psum x1, waiting for transfers between devices, on_device(): lax.psum(jnp.dot(picker, unembed, preferred_element_type=jnp.float32), ('...  452 us
    all_gather x1, blocking collectives, on_device(): tall_block = lax.all_gather(lowered_block, 'feat', axis=0, tiled=True)  195 us
    all_to_all x1, waiting for transfers between devices, on_device(): lax.all_to_all(jnp.stack([tall_block] * lax.axis_size('mp'), 0), axis_nam...  76.1 us
    all_to_all x1, starting transfers between devices, on_device(): lax.all_to_all(jnp.stack([tall_block] * lax.axis_size('mp'), 0), axis_nam...  32.5 us
  transfers between devices with their start and end apart: 2, of which 2 were waited for; matrix products, arithmetic and copies ran while one was open for 1% of the time, Pallas kernels for 0%

profile of v2, /device:TPU:1, one launch (start us, length us, event | category | flops | bytes accessed | tf_op | source)
XLA Modules:
  0.0 805.6 jit_solution(8662714020569655093)
XLA Ops:
  6.5 0.0 copy-start
  6.5 0.0 copy-start.8
  6.5 0.0 copy-start.7
  6.5 0.0 all-reduce.2.cloned.1.call-start
  6.6 1.2 copy-done
  7.8 0.0 copy-start.1
  7.8 1.7 fusion.23
  9.5 0.0 all-reduce.2.cloned.1.call-update
  9.6 1.2 multiply_reduce_fusion
  10.8 1.2 divide_bitcast_fusion
  12.0 0.1 copy.23
  12.1 0.2 reshape.183
  12.3 0.1 constant_dynamic-slice_fusion
  12.4 0.1 copy.24
  12.4 0.0 copy-done.8
  12.5 0.1 fusion.27
  12.5 0.1 reshape.189
  12.6 0.0 copy-done.7
  12.6 0.1 reshape.182
  12.7 0.8 dynamic_slice.15
  13.5 0.1 dynamic-slice
  13.6 0.1 dynamic-slice_bitcast_fusion
  13.6 452.4 %all-reduce.2.cloned.1.call-done = f32[16,2304]{1,0:T(8,128)} async-done(((f32[16,2304]{1,0:T(8,128)}), f32[16,2304]{1,0:T(8,128)}) %all-reduce.2.cloned.1.call-update) | async-done | bytes 147472 | tf_op jit(solution)/shard_map/psum | solution.py:34
  466.0 0.0 copy-start.4
  466.0 2.9 fusion
  468.9 0.0 copy-done.1
  468.9 0.4 fusion.11
  469.3 13.9 %all-gather.1 = bf16[8,12,256]{2,1,0:T(8,128)(2,1)S(1)} all-gather(bf16[1,12,256]{2,1,0:T(8,128)(2,1)S(1)} %fusion.11), channel_id=2, replica_groups=mesh['mp'=8,'feat'=64] {'mp'}, dimensions={0}, use_global_device_ids=true | all-gather | bytes 55296 | tf_op jit(solution)/shard_map/all_gather | solution.py:66
  483.1 0.0 copy-done.4
  483.1 0.0 copy-start.3
  483.2 0.5 mul.102
  483.7 0.5 copy-done.3
  484.2 0.1 broadcast_in_dim.2
  484.3 0.4 fusion.7
  484.7 195.5 %all-gather.2 = bf16[64,12,288]{2,1,0:T(8,128)(2,1)S(1)} all-gather(bf16[1,12,288]{2,1,0:T(8,128)(2,1)S(1)} %fusion.7), channel_id=1, replica_groups=mesh['mp'=8,'feat'=64] {'feat'}, dimensions={0}, use_global_device_ids=true | all-gather | bytes 449280 | tf_op jit(solution)/shard_map/all_gather | solution.py:81
  680.2 0.3 reshape.194
  680.5 0.2 copy.25
  680.7 2.0 stack.2
  682.8 0.0 copy-start.2
  682.8 0.0 copy-start.6
  682.8 32.5 %all-to-all-start = ((bf16[8,768,288]{1,2,0:T(8,128)(2,1)}), bf16[8,768,288]{1,2,0:T(8,128)(2,1)}, u32[]{:S(2)}, u32[]{:S(2)}) async-start(bf16[8,768,288]{1,2,0:T(8,128)(2,1)} %stack.2), calls=%async_computation | async-start | bytes 7077888 | tf_op jit(solution)/shard_map/all_to_all | solution.py:83
  715.3 0.0 copy-done.2
  715.3 0.0 copy-done.6
  715.3 0.1 convert_multiply_fusion
  715.4 0.2 copy.26
  715.6 0.0 copy-start.5
  715.6 0.5 multiply_convert_fusion
  716.2 0.9 copy-done.5
  717.1 1.3 fusion.14
  718.4 76.1 %all-to-all-done = bf16[8,768,288]{1,2,0:T(8,128)(2,1)} async-done(((bf16[8,768,288]{1,2,0:T(8,128)(2,1)}), bf16[8,768,288]{1,2,0:T(8,128)(2,1)}, u32[]{:S(2)}, u32[]{:S(2)}) %all-to-all-start) | async-done | bytes 3538976 | tf_op jit(solution)/shard_map/all_to_all | solution.py:83
  794.5 3.1 fusion.1
  797.6 1.1 copy.27
  (4 shorter events, 0.0 us)
Async XLA Ops:
  6.5 1.3 copy-start
  6.5 5.9 copy-start.8
  6.5 6.1 copy-start.7
  6.5 459.5 %all-reduce.2.cloned.1.call-start = ((), (), s32[]{:S(2)}) async-start(), calls=%async_computation.1 | async-start | bytes 294912 | tf_op jit(solution)/shard_map/psum | solution.py:34
  7.8 461.1 %copy-start.1 = (bf16[1,256,2304]{2,1,0:T(8,128)(2,1)S(1)}, bf16[1,256,2304]{2,1,0:T(8,128)(2,1)}, u32[]{:S(2)}) copy-start(bf16[1,256,2304]{2,1,0:T(8,128)(2,1)} %param.18) | copy-start | bytes 3538948
  466.0 17.1 %copy-start.4 = (f32[16,2304]{1,0:T(8,128)S(1)}, f32[16,2304]{1,0:T(8,128)}, u32[]{:S(2)}) copy-start(f32[16,2304]{1,0:T(8,128)} %all-reduce.2.cloned.1.call-done) | copy-start | bytes 442372
  483.1 1.1 copy-start.3
  682.8 32.5 %copy-start.2 = (s32[16,48,192]{2,1,0:T(8,128)S(1)}, s32[16,48,192]{2,1,0:T(8,128)}, u32[]{:S(2)}) copy-start(s32[16,48,192]{2,1,0:T(8,128)} %param.21) | copy-start | bytes 1769476
  682.8 32.5 %copy-start.6 = (bf16[16,48,192]{2,1,0:T(8,128)(2,1)S(1)}, bf16[16,48,192]{2,1,0:T(8,128)(2,1)}, u32[]{:S(2)}) copy-start(bf16[16,48,192]{2,1,0:T(8,128)(2,1)} %param.20) | copy-start | bytes 884740
  682.8 111.7 %all-to-all-start = ((bf16[8,768,288]{1,2,0:T(8,128)(2,1)}), bf16[8,768,288]{1,2,0:T(8,128)(2,1)}, u32[]{:S(2)}, u32[]{:S(2)}) async-start(bf16[8,768,288]{1,2,0:T(8,128)(2,1)} %stack.2), calls=%async_computation | async-start | bytes 7077888 | tf_op jit(solution)/shard_map/all_to_all | solution.py:83
  715.6 1.5 copy-start.5
Sparse Core Ops, SparseCore 0:
  12.8 453.1 all-reduce.1
